TPU v7x, 256 devices: a whole 4x4x8 slice. The times are simulated.
256 devices in a mesh: song: 4 (over y), seq: 64 (over z, x, core).
Axes of the slice: x: 4, y: 4, z: 8, core: 2. Of those that a mesh axis runs over, the one named last changes fastest.
Arguments:
- queries: bfloat16 [4, 8192, 2048], P('song', 'seq'), may hold values from -64 to 64
- keys: bfloat16 [4, 8192, 2048], P('song', 'seq'), may hold values from -64 to 64
- values: bfloat16 [4, 8192, 2048], P('song', 'seq'), may hold values from -6 to 6
- lyric_keys: bfloat16 [4, 384, 2048], P('song', 'seq'), may hold values from -64 to 64
- lyric_values: bfloat16 [4, 384, 2048], P('song', 'seq'), may hold values from -6 to 6
- q_gain: float32 [128], replicated, may hold values from 0.5 to 1.5
- k_gain: float32 [128], replicated, may hold values from 0.5 to 1.5
- cotangent: bfloat16 [4, 8192, 2048], P('song', 'seq'), may hold values from -12 to 12
- alignment: int32 [4, 64, 2], P('song', 'seq'), may hold values from -1 to 2, as said below
- lyric_len: int32 [4], P('song'), may hold values from 192 to 384
Outputs:
- attn_out: bfloat16 [4, 8192, 2048], P('song', 'seq')
- grad_queries: bfloat16 [4, 8192, 2048], P('song', 'seq')
- grad_keys: bfloat16 [4, 8192, 2048], P('song', 'seq')
- grad_values: bfloat16 [4, 8192, 2048], P('song', 'seq')
- grad_lyric_keys: bfloat16 [4, 384, 2048], P('song', 'seq')
- grad_lyric_values: bfloat16 [4, 384, 2048], P('song', 'seq')
- grad_q_gain: float32 [128], replicated
- grad_k_gain: float32 [128], replicated
Inputs may be any that keep to these rules, and one draw needn't show every extreme that they name: `alignment`: in each row the entries that are not -1 are distinct.
All inputs are finite; a program needn't handle non-finite values.
Results may differ from a plain program's by a relative error of at most 0.01.
Values may be sent and summed in bfloat16 or wider, within the bound.
A program may use at most 128 MiB of HBM per device.

v0:
```python
import jax
import jax.numpy as jnp
from jax import lax
from jax.sharding import PartitionSpec as P

BLK = 128
WIN = 1
TILES = 2
NORM_EPS = 1e-06


def extended_2(block, sides, width):
    for axis, dim in sides:
        count = lax.axis_size(axis)
        forward = [(i, i + 1) for i in range(count - 1)]
        backward = [(target, source) for source, target in forward]
        low = lax.ppermute(
            lax.slice_in_dim(block, block.shape[dim] - width, None, axis=dim), axis, forward
        )
        high = lax.ppermute(lax.slice_in_dim(block, 0, width, axis=dim), axis, backward)
        block = jnp.concatenate([low, block, high], axis=dim)
    return block


def norm_heads(inputs, norm_gain):
    row_values = inputs.astype(jnp.float32).reshape(inputs.shape[0], -1, norm_gain.shape[0])
    inverse = lax.rsqrt(jnp.mean(row_values * row_values, axis=-1, keepdims=True) + NORM_EPS)
    return (row_values * inverse * norm_gain, inverse)


def norm_back(inputs, inverse, norm_gain, grad_out):
    row_values = inputs.astype(jnp.float32).reshape(grad_out.shape)
    scaled = grad_out * norm_gain
    grad_input = inverse * scaled - row_values * inverse * inverse * inverse * jnp.mean(
        scaled * row_values, axis=-1, keepdims=True
    )
    grad_gain = jnp.sum(grad_out * row_values * inverse, axis=(0, 1))
    return (grad_input.reshape(inputs.shape), grad_gain)


def block_pass(query_rows, key_rows, value_rows, keep_mask, grad_rows, score_scale):
    scores = (
        jnp.einsum("qhd,khd->hqk", query_rows, key_rows, preferred_element_type=jnp.float32)
        * score_scale
    )
    exp_scores = jnp.where(keep_mask[None, None, :], jnp.exp(scores), 0.0)
    totals = jnp.sum(exp_scores, axis=2)
    prob_full = exp_scores / totals[:, :, None]
    prob_low = prob_full.astype(jnp.bfloat16)
    block_output = jnp.einsum(
        "hqk,khd->qhd", prob_low, value_rows, preferred_element_type=jnp.float32
    ).astype(jnp.bfloat16)
    delta_rows = jnp.sum(grad_rows.astype(jnp.float32) * block_output.astype(jnp.float32), axis=2).T
    grad_prob = jnp.einsum(
        "qhd,khd->hqk", grad_rows, value_rows, preferred_element_type=jnp.float32
    )
    grad_score = (prob_full * (grad_prob - delta_rows[:, :, None])).astype(jnp.bfloat16)
    query_gradient = (
        jnp.einsum("hqk,khd->qhd", grad_score, key_rows, preferred_element_type=jnp.float32)
        * score_scale
    )
    grad_key = (
        jnp.einsum("hqk,qhd->khd", grad_score, query_rows, preferred_element_type=jnp.float32)
        * score_scale
    )
    value_gradient = jnp.einsum(
        "hqk,qhd->khd", prob_low, grad_rows, preferred_element_type=jnp.float32
    )
    return (block_output, query_gradient, grad_key, value_gradient)


def body(
    queries, keys, values, lyric_keys, lyric_values, q_gain, k_gain, cotangent, alignment, lyric_len
):
    head_size = q_gain.shape[0]
    model_width = queries.shape[2]
    head_count = model_width // head_size
    frames = queries.shape[1]
    lyric_local = lyric_keys.shape[1]
    seq_count = lax.axis_size("seq")
    border_rows = WIN * BLK
    window_extent = (2 * WIN + 1) * BLK
    score_scale = head_size ** (-0.5)
    total_frames = frames * seq_count
    first_frame = lax.axis_index("seq") * frames
    lyric_total = lyric_local * seq_count
    lyric_blocks = lyric_total // BLK
    lyric_pair = jnp.stack([lyric_keys[0], lyric_values[0]])
    lyric_all = lax.all_gather(lyric_pair, "seq", axis=1, tiled=True)
    lyric_raw_all = lyric_all[0]
    lyric_val_all = lyric_all[1].reshape(lyric_total, head_count, head_size)
    query_raw = queries[0]
    key_raw = keys[0]
    query_full, query_inv = norm_heads(query_raw, q_gain)
    key_full, key_inv = norm_heads(key_raw, k_gain)
    lyric_full_all, lyric_inv_all = norm_heads(lyric_raw_all, k_gain)
    lyric_inv = norm_heads(lyric_keys[0], k_gain)[1]
    query_norm = query_full.astype(jnp.bfloat16)
    key_norm = key_full.astype(jnp.bfloat16)
    lyric_key_all = lyric_full_all.astype(jnp.bfloat16)
    stacked = jnp.stack([key_norm.reshape(frames, model_width), values[0]])
    extended = extended_2(stacked, (("seq", 1),), border_rows)
    ext_keys = extended[0].reshape(frames + 2 * border_rows, head_count, head_size)
    ext_vals = extended[1].reshape(frames + 2 * border_rows, head_count, head_size)
    grad_heads = cotangent[0].reshape(frames, head_count, head_size)
    length = lyric_len[0]
    position = first_frame - border_rows + jnp.arange(window_extent, dtype=jnp.int32)
    audio_mask = (position >= 0) & (position < total_frames)
    tile_ids = alignment[0, 0]
    starts = [jnp.maximum(tile_ids[s], 0) * BLK for s in range(TILES)]
    slot_keys = [lax.dynamic_slice_in_dim(lyric_key_all, st, BLK, 0) for st in starts]
    slot_vals = [lax.dynamic_slice_in_dim(lyric_val_all, st, BLK, 0) for st in starts]
    lyric_mask = jnp.concatenate(
        [
            (tile_ids[s] >= 0) & (starts[s] + jnp.arange(BLK, dtype=jnp.int32) < length)
            for s in range(TILES)
        ]
    )
    all_keys = jnp.concatenate([ext_keys] + slot_keys, axis=0)
    all_vals = jnp.concatenate([ext_vals] + slot_vals, axis=0)
    keep_mask = jnp.concatenate([audio_mask, lyric_mask], axis=0)
    block_output, grad_qn, grad_key, value_gradient = block_pass(
        query_norm, all_keys, all_vals, keep_mask, grad_heads, score_scale
    )
    lyric_gk = grad_key[window_extent:].reshape(TILES, BLK, head_count, head_size)
    lyric_gv = value_gradient[window_extent:].reshape(TILES, BLK, head_count, head_size)
    block_ids = jnp.arange(lyric_blocks, dtype=jnp.int32)
    pick = [(tile_ids[s] == block_ids)[:, None, None, None] for s in range(TILES)]
    part_gk = sum((jnp.where(pick[s], lyric_gk[s][None], 0.0) for s in range(TILES)))
    part_gv = sum((jnp.where(pick[s], lyric_gv[s][None], 0.0) for s in range(TILES)))
    lyric_scaled_all = lyric_raw_all.astype(jnp.float32).reshape(
        lyric_blocks, BLK, head_count, head_size
    ) * lyric_inv_all.reshape(lyric_blocks, BLK, head_count, 1)
    lyric_gain_vector = jnp.sum(part_gk * lyric_scaled_all, axis=(0, 1, 2))
    parts = jnp.stack([part_gk, part_gv]).reshape(2, seq_count, lyric_local * model_width)
    summed = lax.psum_scatter(parts, "seq", scatter_dimension=1, tiled=True)
    summed_key = summed[0].reshape(lyric_local, head_count, head_size)
    summed_val = summed[1].reshape(lyric_local, model_width)
    ext_grad_key = grad_key[:window_extent]
    ext_grad_val = value_gradient[:window_extent]
    own_grad_key = ext_grad_key[border_rows : border_rows + frames]
    own_grad_val = ext_grad_val[border_rows : border_rows + frames]
    rims = jnp.stack(
        [
            jnp.concatenate(
                [ext_grad_key[:border_rows], ext_grad_key[border_rows + frames :]], axis=0
            ).reshape(2 * border_rows, model_width),
            jnp.concatenate(
                [ext_grad_val[:border_rows], ext_grad_val[border_rows + frames :]], axis=0
            ).reshape(2 * border_rows, model_width),
        ]
    )
    received = extended_2(rims.astype(jnp.bfloat16), (("seq", 1),), border_rows).astype(rims.dtype)
    from_left = received[:, :border_rows].reshape(2, border_rows, head_count, head_size)
    from_right = received[:, 3 * border_rows :].reshape(2, border_rows, head_count, head_size)
    own_grad_key = (
        own_grad_key.at[:border_rows]
        .add(from_left[0])
        .at[frames - border_rows :]
        .add(from_right[0])
    )
    own_grad_val = (
        own_grad_val.at[:border_rows]
        .add(from_left[1])
        .at[frames - border_rows :]
        .add(from_right[1])
    )
    unnormed_query_gradient, query_gain_vector = norm_back(
        query_raw, query_inv, q_gain, grad_qn.reshape(frames, head_count, head_size)
    )
    unnormed_key_gradient, key_gain_vector = norm_back(key_raw, key_inv, k_gain, own_grad_key)
    total_gains = lax.psum(
        jnp.stack([query_gain_vector, key_gain_vector + lyric_gain_vector]), ("song", "seq")
    )
    unnormed_lyric_gradient = norm_back(lyric_keys[0], lyric_inv, k_gain, summed_key)[0]
    return (
        block_output.reshape(1, frames, model_width),
        unnormed_query_gradient.astype(jnp.bfloat16)[None],
        unnormed_key_gradient.astype(jnp.bfloat16)[None],
        own_grad_val.reshape(1, frames, model_width).astype(jnp.bfloat16),
        unnormed_lyric_gradient.astype(jnp.bfloat16)[None],
        summed_val.astype(jnp.bfloat16)[None],
        total_gains[0],
        total_gains[1],
    )


def solution(mesh):
    in_specs = (
        P("song", "seq", None),
        P("song", "seq", None),
        P("song", "seq", None),
        P("song", "seq", None),
        P("song", "seq", None),
        P(),
        P(),
        P("song", "seq", None),
        P("song", "seq", None),
        P("song"),
    )
    out_specs = (
        P("song", "seq", None),
        P("song", "seq", None),
        P("song", "seq", None),
        P("song", "seq", None),
        P("song", "seq", None),
        P("song", "seq", None),
        P(),
        P(),
    )
    return jax.shard_map(body, mesh=mesh, in_specs=in_specs, out_specs=out_specs, check_vma=False)
```

profile of v0, /device:TPU:8, one launch (start us, length us, event | category | flops | bytes accessed | tf_op | source)
XLA Modules:
  0.0 408.7 jit_solution(17352905032902719818)
XLA Ops:
  15.9 4.0 collective-permute-start
  26.2 2.0 pad_maximum_fusion.1
  31.3 61.3 %all-gather.2.cloned.1.call-done = bf16[2,384,2048]{2,0,1:T(2,128)(2,1)} async-done(((bf16[2,6,2048]{2,0,1:T(2,128)(2,1)}), bf16[2,384,2048]{2,0,1:T(2,128)(2,1)}) %all-gather.2.cloned.1.call-update) | async-done | bytes 3145744 | tf_op jit(solution)/shard_map/all_gather | solution.py:89
  92.6 9.6 %fusion.43 = (bf16[1,384,2048]{2,0,1:T(2,128)(2,1)}, bf16[1,384,2048]{2,0,1:T(2,128)(2,1)}) fusion(bf16[2,384,2048]{2,0,1:T(2,128)(2,1)} %all-gather.2.cloned.1.call-done), kind=kLoop, calls=%fused_computation.109 | loop fusion | bytes 6291456 | tf_op jit(solution)/shard_map/slice | solution.py:90
  102.1 6.9 %copy.192 = bf16[1,384,2048]{1,2,0:T(8,128)(2,1)S(1)} copy(bf16[1,384,2048]{2,0,1:T(2,128)(2,1)} %get-tuple-element.169) | data formatting | bytes 3145728
  109.1 2.1 copy.165
  111.6 6.9 %copy.162 = bf16[1,384,2048]{1,2,0:T(8,128)(2,1)S(1)} copy(bf16[1,384,2048]{2,0,1:T(2,128)(2,1)} %get-tuple-element.170) | data formatting | bytes 3145728 | tf_op jit(solution)/shard_map/slice | solution.py:91
  118.5 2.4 multiply_convert_fusion
  124.3 3.1 fusion.48
  127.5 2.4 multiply_reduce_fusion.4
  129.9 2.2 fusion
  132.1 3.3 fusion.47
  136.3 1.7 fusion.11
  139.3 4.0 collective-permute-start.2
  145.3 3.3 maximum_convert_fusion
  153.4 3.7 fusion.41
  159.9 4.5 %select_add_fusion.1 = (f32[3,128,16,128]{3,2,1,0:T(8,128)S(1)}, f32[3,128,16,128]{3,2,1,0:T(8,128)}) fusion(f32[128,16,128]{2,1,0:T(8,128)} %copy.174, f32[128,16,128]{2,1,0:T(8,128)} %copy.173, pred[3]{0:T(512)(128)(4,1)S(1)} %get-tuple-element.198, pred[3]{0:T(512)(128)(4,1)S(1)} %get-tuple-element.199, f32[128,16,128]{2,1,0:T(8,128)} %copy.176, ...), kind=kLoop, calls=%fused_computation.10 | loop fusion | flops 4718592 | bytes 10485766 | tf_op jit(solution)/shard_map/add | solution.py:129
  164.5 4.3 %add.181 = f32[1,64,12288]{2,1,0:T(8,128)} reshape(f32[3,128,16,128]{3,2,1,0:T(8,128)} %get-tuple-element.184) | data formatting | bytes 6291456 | tf_op jit(solution)/shard_map/add | solution.py:130
  168.8 1.9 add.179
  170.7 3.3 pad_maximum_fusion
  174.0 7.5 %copy.177 = f32[2,64,12288]{2,0,1:T(2,128)} copy(f32[2,64,12288]{2,1,0:T(8,128)S(1)} %pad_maximum_fusion) | data formatting | bytes 12582912 | tf_op jit(solution)/shard_map/stack | solution.py:135
  183.6 3.2 fusion.16
  189.0 2.3 mul.400
  191.4 3.7 copy.181
  198.9 2.3 broadcast_in_dim.118
  201.1 3.5 copy.179
  206.2 2.3 broadcast_in_dim.113
  208.5 3.7 copy.178
  212.2 4.6 %multiply_reduce_fusion = f32[2048]{0:T(1024)S(1)} fusion(f32[1,384,2048]{1,2,0:T(8,128)} %copy.181, f32[1,384,2048]{1,2,0:T(8,128)} %copy.179, f32[1,384,2048]{1,2,0:T(8,128)} %copy.178, pred[384]{0:T(512)(128)(4,1)S(1)} %broadcast_bitcast_fusion.1, pred[384]{0:T(512)(128)(4,1)S(1)} %broadcast_bitcast_fusion.2, bf16[1,384,2048]{1,2,0:T(8,128)(2,1)S(1)} %copy-done.1), kind=kLoop, calls=%fused_computation.8 | loop fusion | flops 5502976 | bytes 11019008 | tf_op jit(solution)/shard_map/reduce_sum | solution.py:134
  216.9 88.1 %psum.7 = f32[2,128]{1,0:T(2,128)S(1)} all-reduce(f32[2,128]{1,0:T(2,128)S(1)} %pad_maximum_fusion.16), channel_id=1, replica_groups=mesh['song'=4,'seq'=64] {'song','seq'}, use_global_device_ids=true, to_apply=%region_14.15 | all-reduce | flops 256 | bytes 2048 | tf_op jit(solution)/shard_map/psum | solution.py:172
  305.5 90.2 %all-reduce.3.cloned.1.call-done = f32[2,64,12288]{2,0,1:T(2,128)} async-done(((f32[2,64,12288]{2,0,1:T(2,128)}), f32[2,64,12288]{2,0,1:T(2,128)}) %all-reduce.3.cloned.1.call-update) | async-done | bytes 6291472
  396.2 2.3 fusion.38
  (127 shorter events, 44.1 us)
Async XLA Ops:
  7.2 85.4 %all-gather.2.cloned.1.call-start = ((), (), s32[]{:S(2)}) async-start(), calls=%async_computation | async-start | bytes 3194880 | tf_op jit(solution)/shard_map/all_gather | solution.py:89
  9.6 386.1 %all-reduce.3.cloned.1.call-start = ((), (), s32[]{:S(2)}) async-start(), calls=%async_computation.1 | async-start | bytes 12582912
  10.9 9.0 %copy-start.19 = (s32[1,1,2]{2,1,0:T(1,128)S(1)}, s32[1,1,2]{2,1,0:T(1,128)}, u32[]{:S(2)}) copy-start(s32[1,1,2]{2,1,0:T(1,128)} %param.34) | copy-start | bytes 28
  11.0 12.2 %copy-start.12 = (bf16[1,128,2048]{2,1,0:T(8,128)(2,1)S(1)}, bf16[1,128,2048]{2,1,0:T(8,128)(2,1)}, u32[]{:S(2)}) copy-start(bf16[1,128,2048]{2,1,0:T(8,128)(2,1)} %param.33) | copy-start | bytes 1572868
  14.6 11.6 %collective-permute-start.1 = (bf16[2,128,2048]{1,2,0:T(8,128)(2,1)S(1)}, bf16[2,128,2048]{1,2,0:T(8,128)(2,1)}, u32[]{:S(2)}, u32[]{:S(2)}) collective-permute-start(bf16[2,128,2048]{1,2,0:T(8,128)(2,1)S(1)} %pad_maximum_fusion.9), channel_id=1, source_target_pairs={{1,0},{2,1},{3,2},{4,3},{5,4},{6,5},{7,6},{8,7},{9,8},{10,9},{11,1... | collective-permute-start | bytes 3145736 | tf_op jit(solution)/shard_map/ppermute | solution.py:20
  15.9 10.3 %collective-permute-start = (bf16[2,128,2048]{1,2,0:T(8,128)(2,1)S(1)}, bf16[2,128,2048]{1,2,0:T(8,128)(2,1)}, u32[]{:S(2)}, u32[]{:S(2)}) collective-permute-start(bf16[2,128,2048]{1,2,0:T(8,128)(2,1)S(1)} %pad_maximum_fusion.9), channel_id=1, source_target_pairs={{0,1},{1,2},{2,3},{3,4},{4,5},{5,6},{6,7},{7,8},{8,9},{9,10},{10,1... | collective-permute-start | bytes 3145736 | tf_op jit(solution)/shard_map/ppermute | solution.py:17
  26.0 106.0 %copy-start.2 = (f32[1,128,2048]{1,2,0:T(8,128)}, f32[1,128,2048]{1,2,0:T(8,128)S(1)}, u32[]{:S(2)}) copy-start(f32[1,128,2048]{1,2,0:T(8,128)S(1)} %copy.163) | copy-start | bytes 3145732
  109.1 2.5 copy-start
  111.2 7.3 %copy-start.18 = (f32[128]{0:T(128)S(1)}, f32[128]{0:T(128)}, u32[]{:S(2)}) copy-start(f32[128]{0:T(128)} %param.32) | copy-start | bytes 1540
  120.9 1.8 copy-start.9
  121.0 1.8 copy-start.20
  121.1 3.2 copy-start.15
  121.1 3.2 copy-start.16
  122.7 1.6 copy-start.14
  124.3 3.1 copy-start.11
  132.1 3.3 copy-start.7
  136.1 7.2 %copy-start.21 = (u32[256]{0:T(256)S(1)}, u32[256]{0:T(256)}, u32[]{:S(2)}) copy-start(u32[256]{0:T(256)} %constant.174) | copy-start | bytes 3076
  136.3 12.3 %slice-start = ((s8[5242880]{0:T(1024)(128)(4,1)}), s8[1048576]{0:T(1024)(128)(4,1)S(1)}, s32[]{:S(2)}) async-start(s8[5242880]{0:T(1024)(128)(4,1)} %bitcast.106), calls=%async_computation.2 | async-start | bytes 2097152
  138.0 7.3 %collective-permute-start.3 = (bf16[2,128,2048]{1,2,0:T(8,128)(2,1)}, bf16[2,128,2048]{1,2,0:T(8,128)(2,1)}, u32[]{:S(2)}, u32[]{:S(2)}) collective-permute-start(bf16[2,128,2048]{1,2,0:T(8,128)(2,1)} %get-tuple-element.176), channel_id=1, source_target_pairs={{1,0},{2,1},{3,2},{4,3},{5,4},{6,5},{7,6},{8,7},{9,8},{10,9},{11,1... | collective-permute-start | bytes 3145736 | tf_op jit(solution)/shard_map/ppermute | solution.py:20
  139.3 6.0 %collective-permute-start.2 = (bf16[2,128,2048]{1,2,0:T(8,128)(2,1)}, bf16[2,128,2048]{1,2,0:T(8,128)(2,1)}, u32[]{:S(2)}, u32[]{:S(2)}) collective-permute-start(bf16[2,128,2048]{1,2,0:T(8,128)(2,1)} %get-tuple-element.175), channel_id=1, source_target_pairs={{0,1},{1,2},{2,3},{3,4},{4,5},{5,6},{6,7},{7,8},{8,9},{9,10},{10,1... | collective-permute-start | bytes 3145736 | tf_op jit(solution)/shard_map/ppermute | solution.py:17
  145.3 3.3 slice-start.1
  145.3 3.7 copy-start.4
  181.5 0.8 copy-start.17
  181.5 1.1 copy-start.13
  181.5 2.1 copy-start.3
  181.5 2.1 copy-start.10
  191.3 3.7 copy-start.5
  191.3 3.7 copy-start.6
  195.0 1.4 copy-start.8
  208.5 3.7 copy-start.1
Sparse Core Ops, SparseCore 0:
  11.3 81.1 all-gather.1
  181.6 213.9 all-reduce.2
where the time goes:
time: 410 us; the launch traced here: 409 us
  waiting for transfers between devices  152 us (37%)
  local copies, waits for them, and re-layouts  91.8 us (22%)
  blocking collectives  88.1 us (21%)
  other arithmetic  32.9 us (8%)
  between operations  17.9 us (4%)
  matrix products  15.8 us (4%)
  starting transfers between devices  10.7 us (3%)
    unnamed x3, waiting for transfers between devices  90.2 us
    psum x1, blocking collectives, body(): lax.psum(jnp.stack([query_gain_vector, key_gain_vector + lyric_gain_vecto...  88.1 us
    all_gather x1, waiting for transfers between devices, body(): lyric_all = lax.all_gather(lyric_pair, 'seq', axis=1, tiled=True)  61.3 us
    unnamed x59, local copies, waits for them, and re-layouts  19.6 us
    broadcast_in_dim x8, local copies, waits for them, and re-layouts, body(): jnp.where(pick[s], lyric_gk[s][None], 0.0)  15 us
    slice x1, local copies, waits for them, and re-layouts, body(): lyric_raw_all = lyric_all[0]  9.57 us
  transfers between devices with their start and end apart: 6, of which 2 were waited for; matrix products, arithmetic and copies ran while one was open for 12% of the time, Pallas kernels for 0%

commit v1 on v0

--- a/solution.py
+++ b/solution.py
@@ -86,7 +86,9 @@
     lyric_total = lyric_local * seq_count
     lyric_blocks = lyric_total // BLK
     lyric_pair = jnp.stack([lyric_keys[0], lyric_values[0]])
-    lyric_all = lax.all_gather(lyric_pair, "seq", axis=1, tiled=True)
+    lyric_all = jnp.concatenate(
+        lax.all_to_all(jnp.stack([lyric_pair] * lax.axis_size("seq")), "seq", 0, 0), axis=1
+    )
     lyric_raw_all = lyric_all[0]
     lyric_val_all = lyric_all[1].reshape(lyric_total, head_count, head_size)
     query_raw = queries[0]

time: 410 us -> 423 us (1.032)
  local copies, waits for them, and re-layouts: 91.8 us -> 58.1 us
  other arithmetic: 32.9 us -> 50.1 us
  blocking collectives: 88.1 us -> 103 us
  starting transfers between devices: 10.7 us -> 23 us
    all_gather x1 -> x0, waiting for transfers between devices: 61.3 us -> none  [body(): lyric_all = lax.all_gather(lyric_pair, 'seq', axis=1, tiled=True)]
    all_to_all x0 -> x1, waiting for transfers between devices: none -> 54.8 us  [body(): lax.all_to_all(jnp.stack([lyric_pair] * lax.axis_size('seq')), 'seq', 0, 0)]
    slice x2 -> x0, local copies, waits for them, and re-layouts: 16.5 us -> none  [the longest x1 9.57 us: body(): lyric_raw_all = lyric_all[0]]
    psum x1, blocking collectives: 88.1 us -> 103 us  [body(): lax.psum(jnp.stack([query_gain_vector, key_gain_vector + lyric_gain_vecto...]
    all_to_all x0 -> x1, starting transfers between devices: none -> 12.3 us  [body(): lax.all_to_all(jnp.stack([lyric_pair] * lax.axis_size('seq')), 'seq', 0, 0)]
    unnamed x59 -> x50, local copies, waits for them, and re-layouts: 19.6 us -> 9.28 us
    unnamed x3 -> x2, waiting for transfers between devices: 90.2 us -> 97.8 us
    another operation x1, other arithmetic: 3.29 us -> 10.8 us  [body(): jnp.stack([part_gk, part_gv])]
  transfers between devices with their start and end apart: 6 -> 6, of which waited for: 2 -> 2; matrix products, arithmetic and copies ran while one was open for 12% -> 9% of each run, Pallas kernels for 0% -> 0%
where the time goes in v1:
time: 423 us; the launch traced here: 422 us
  waiting for transfers between devices  153 us (36%)
  blocking collectives  103 us (24%)
  local copies, waits for them, and re-layouts  58.1 us (14%)
  other arithmetic  50.1 us (12%)
  starting transfers between devices  23 us (5%)
  between operations  17.9 us (4%)
  matrix products  17.4 us (4%)
    psum x1, blocking collectives, body(): lax.psum(jnp.stack([query_gain_vector, key_gain_vector + lyric_gain_vecto...  103 us
    unnamed x2, waiting for transfers between devices  97.8 us
    all_to_all x1, waiting for transfers between devices, body(): lax.all_to_all(jnp.stack([lyric_pair] * lax.axis_size('seq')), 'seq', 0, 0)  54.8 us
    all_to_all x1, starting transfers between devices, body(): lax.all_to_all(jnp.stack([lyric_pair] * lax.axis_size('seq')), 'seq', 0, 0)  12.3 us
    another operation x1, other arithmetic, body(): jnp.stack([part_gk, part_gv])  10.8 us
    unnamed x50, local copies, waits for them, and re-layouts  9.28 us
  transfers between devices with their start and end apart: 6, of which 2 were waited for; matrix products, arithmetic and copies ran while one was open for 9% of the time, Pallas kernels for 0%

profile of v1, /device:TPU:8, one launch (start us, length us, event | category | flops | bytes accessed | tf_op | source)
XLA Modules:
  0.0 422.2 jit_solution(11906015357980051999)
XLA Ops:
  8.0 4.7 %stack.17 = bf16[64,2,6,2048]{3,1,2,0:T(2,128)(2,1)} broadcast(bf16[2,6,2048]{2,0,1:T(2,128)(2,1)S(1)} %copy.163), dimensions={1,2,3} | broadcast | bytes 3194880 | tf_op jit(solution)/shard_map/stack | solution.py:90
  12.7 12.3 %all-to-all-start = ((bf16[64,2,6,2048]{3,1,2,0:T(2,128)(2,1)}), bf16[64,2,6,2048]{3,1,2,0:T(2,128)(2,1)}, u32[]{:S(2)}, u32[]{:S(2)}) async-start(bf16[64,2,6,2048]{3,1,2,0:T(2,128)(2,1)} %stack.17), calls=%async_computation | async-start | bytes 6291456 | tf_op jit(solution)/shard_map/all_to_all | solution.py:90
  28.6 4.0 collective-permute-start
  44.0 54.8 %all-to-all-done = bf16[64,2,6,2048]{3,1,2,0:T(2,128)(2,1)} async-done(((bf16[64,2,6,2048]{3,1,2,0:T(2,128)(2,1)}), bf16[64,2,6,2048]{3,1,2,0:T(2,128)(2,1)}, u32[]{:S(2)}, u32[]{:S(2)}) %all-to-all-start) | async-done | bytes 3145760 | tf_op jit(solution)/shard_map/all_to_all | solution.py:90
  98.8 3.5 copy.203
  102.3 3.7 slice_convert_fusion
  106.3 3.4 reshape.558
  110.7 2.7 fusion.4
  113.3 3.5 reshape_squeeze.19
  116.9 2.4 constant_dynamic-slice_fusion.1
  122.2 3.1 fusion.2
  125.4 3.1 fusion.49
  128.5 2.4 multiply_reduce_fusion.4
  130.9 2.1 fusion
  133.1 3.3 fusion.48
  140.3 4.0 collective-permute-start.2
  146.7 3.2 maximum_convert_fusion
  149.9 3.6 fusion.42
  154.0 2.1 copy.177
  156.2 4.5 %fusion.43 = (f32[128,16,128]{0,2,1:T(8,128)}, f32[128,16,128]{0,2,1:T(8,128)}, bf16[128,16,128]{0,2,1:T(8,128)(2,1)}) fusion(f32[640,16,128]{0,2,1:T(8,128)} %get-tuple-element.195, f32[128,16,128]{0,2,1:T(8,128)} %bitcast.109, f32[128,16,128]{0,2,1:T(8,128)} %bitcast.108), kind=kLoop, calls=%fused_computation.109 | loop fusion | flops 786432 | bytes 7864320 | tf_op jit(solution)/shard_map/slice | solution.py:132
  160.7 2.6 copy.180
  163.3 2.6 copy.179
  165.9 3.9 select_add_fusion.1
  169.8 10.8 %pad_maximum_fusion = f32[2,64,12288]{2,0,1:T(2,128)} fusion(f32[1,64,12288]{2,0,1:T(1,128)} %bitcast.101, f32[1,64,12288]{2,0,1:T(1,128)S(1)} %bitcast.100), kind=kLoop, calls=%fused_computation | loop fusion | flops 1572864 | bytes 12582912 | tf_op jit(solution)/shard_map/stack | solution.py:137
  182.6 3.2 fusion.18
  188.4 2.2 mul.400
  196.0 2.2 broadcast_in_dim.118
  199.7 2.2 broadcast_in_dim.113
  201.9 5.9 %multiply_reduce_fusion = f32[2048]{0:T(1024)S(1)} fusion(f32[1,64,6,2048]{3,2,1,0:T(8,128)} %mul.400, f32[1,64,6,2048]{3,2,1,0:T(8,128)} %broadcast_in_dim.118, f32[1,64,6,2048]{3,2,1,0:T(8,128)} %broadcast_in_dim.113, pred[64,6]{1,0:T(8,128)(4,1)S(1)} %broadcast_in_dim.116, pred[64,6]{1,0:T(8,128)(4,1)S(1)} %broadcast_in_dim.111, ...), kind=kLoop, calls=%fused_computation.8 | loop fusion | flops 5502976 | bytes 11019008 | tf_op jit(solution)/shard_map/reduce_sum | solution.py:136
  207.8 103.1 %psum.7 = f32[2,128]{1,0:T(2,128)S(1)} all-reduce(f32[2,128]{1,0:T(2,128)S(1)} %pad_maximum_fusion.16), channel_id=1, replica_groups=mesh['song'=4,'seq'=64] {'song','seq'}, use_global_device_ids=true, to_apply=%region_14.15 | all-reduce | flops 256 | bytes 2048 | tf_op jit(solution)/shard_map/psum | solution.py:174
  311.4 97.8 %all-reduce.3.cloned.1.call-done = f32[2,64,12288]{2,0,1:T(2,128)} async-done(((f32[2,64,12288]{2,0,1:T(2,128)}), f32[2,64,12288]{2,0,1:T(2,128)}) %all-reduce.3.cloned.1.call-update) | async-done | bytes 6291472
  409.7 2.3 fusion.40
  (116 shorter events, 38.9 us)
Async XLA Ops:
  12.7 12.4 %copy-start.10 = (bf16[1,128,2048]{2,1,0:T(8,128)(2,1)S(1)}, bf16[1,128,2048]{2,1,0:T(8,128)(2,1)}, u32[]{:S(2)}) copy-start(bf16[1,128,2048]{2,1,0:T(8,128)(2,1)} %param.28) | copy-start | bytes 1572868
  12.7 12.6 %copy-start.11 = (bf16[1,128,2048]{2,1,0:T(8,128)(2,1)S(1)}, bf16[1,128,2048]{2,1,0:T(8,128)(2,1)}, u32[]{:S(2)}) copy-start(bf16[1,128,2048]{2,1,0:T(8,128)(2,1)} %param.27) | copy-start | bytes 1572868
  12.7 12.9 %copy-start.16 = (f32[128]{0:T(128)S(1)}, f32[128]{0:T(128)}, u32[]{:S(2)}) copy-start(f32[128]{0:T(128)} %param.32) | copy-start | bytes 1540
  12.7 86.0 %all-to-all-start = ((bf16[64,2,6,2048]{3,1,2,0:T(2,128)(2,1)}), bf16[64,2,6,2048]{3,1,2,0:T(2,128)(2,1)}, u32[]{:S(2)}, u32[]{:S(2)}) async-start(bf16[64,2,6,2048]{3,1,2,0:T(2,128)(2,1)} %stack.17), calls=%async_computation | async-start | bytes 6291456 | tf_op jit(solution)/shard_map/all_to_all | solution.py:90
  25.1 384.2 %all-reduce.3.cloned.1.call-start = ((), (), s32[]{:S(2)}) async-start(), calls=%async_computation.1 | async-start | bytes 12582912
  25.4 7.2 %copy-start.17 = (s32[1,1,2]{2,1,0:T(1,128)S(1)}, s32[1,1,2]{2,1,0:T(1,128)}, u32[]{:S(2)}) copy-start(s32[1,1,2]{2,1,0:T(1,128)} %param.34) | copy-start | bytes 28
  25.7 10.1 %copy-start.12 = (bf16[1,128,2048]{2,1,0:T(8,128)(2,1)S(1)}, bf16[1,128,2048]{2,1,0:T(8,128)(2,1)}, u32[]{:S(2)}) copy-start(bf16[1,128,2048]{2,1,0:T(8,128)(2,1)} %param.33) | copy-start | bytes 1572868
  27.3 11.6 %collective-permute-start.1 = (bf16[2,128,2048]{1,2,0:T(8,128)(2,1)S(1)}, bf16[2,128,2048]{1,2,0:T(8,128)(2,1)}, u32[]{:S(2)}, u32[]{:S(2)}) collective-permute-start(bf16[2,128,2048]{1,2,0:T(8,128)(2,1)S(1)} %pad_maximum_fusion.9), channel_id=1, source_target_pairs={{1,0},{2,1},{3,2},{4,3},{5,4},{6,5},{7,6},{8,7},{9,8},{10,9},{11,1... | collective-permute-start | bytes 3145736 | tf_op jit(solution)/shard_map/ppermute | solution.py:20
  28.6 10.3 %collective-permute-start = (bf16[2,128,2048]{1,2,0:T(8,128)(2,1)S(1)}, bf16[2,128,2048]{1,2,0:T(8,128)(2,1)}, u32[]{:S(2)}, u32[]{:S(2)}) collective-permute-start(bf16[2,128,2048]{1,2,0:T(8,128)(2,1)S(1)} %pad_maximum_fusion.9), channel_id=1, source_target_pairs={{0,1},{1,2},{2,3},{3,4},{4,5},{5,6},{6,7},{7,8},{8,9},{9,10},{10,1... | collective-permute-start | bytes 3145736 | tf_op jit(solution)/shard_map/ppermute | solution.py:17
  38.7 2.1 copy-start.1
  102.3 4.0 copy-start
  116.8 5.3 %copy-start.2 = (f32[1,128,2048]{1,2,0:T(8,128)S(1)}, f32[1,128,2048]{1,2,0:T(8,128)}, u32[]{:S(2)}) copy-start(f32[1,128,2048]{1,2,0:T(8,128)} %copy-done.1) | copy-start | bytes 3145732
  116.9 5.3 %copy-start.18 = (f32[128]{0:T(128)S(1)}, f32[128]{0:T(128)}, u32[]{:S(2)}) copy-start(f32[128]{0:T(128)} %param.31) | copy-start | bytes 1540
  122.2 3.2 copy-start.14
  125.3 3.1 copy-start.9
  133.1 3.3 copy-start.6
  137.1 9.0 %copy-start.19 = (u32[256]{0:T(256)S(1)}, u32[256]{0:T(256)}, u32[]{:S(2)}) copy-start(u32[256]{0:T(256)} %constant.174) | copy-start | bytes 3076
  137.1 9.6 %copy-start.15 = (bf16[1,6,2048]{2,1,0:T(8,128)(2,1)S(1)}, bf16[1,6,2048]{2,1,0:T(8,128)(2,1)}, u32[]{:S(2)}) copy-start(bf16[1,6,2048]{2,1,0:T(8,128)(2,1)} %param.29) | copy-start | bytes 73732
  139.0 7.7 %collective-permute-start.3 = (bf16[2,128,2048]{1,2,0:T(8,128)(2,1)}, bf16[2,128,2048]{1,2,0:T(8,128)(2,1)}, u32[]{:S(2)}, u32[]{:S(2)}) collective-permute-start(bf16[2,128,2048]{1,2,0:T(8,128)(2,1)} %get-tuple-element.176), channel_id=1, source_target_pairs={{1,0},{2,1},{3,2},{4,3},{5,4},{6,5},{7,6},{8,7},{9,8},{10,9},{11,1... | collective-permute-start | bytes 3145736 | tf_op jit(solution)/shard_map/ppermute | solution.py:20
  140.3 6.4 %collective-permute-start.2 = (bf16[2,128,2048]{1,2,0:T(8,128)(2,1)}, bf16[2,128,2048]{1,2,0:T(8,128)(2,1)}, u32[]{:S(2)}, u32[]{:S(2)}) collective-permute-start(bf16[2,128,2048]{1,2,0:T(8,128)(2,1)} %get-tuple-element.175), channel_id=1, source_target_pairs={{0,1},{1,2},{2,3},{3,4},{4,5},{5,6},{6,7},{7,8},{8,9},{9,10},{10,1... | collective-permute-start | bytes 3145736 | tf_op jit(solution)/shard_map/ppermute | solution.py:17
  146.7 3.2 copy-start.3
  154.0 11.8 %copy-start.5 = (f32[128,16,128]{2,1,0:T(8,128)}, f32[128,16,128]{2,1,0:T(8,128)S(1)}, u32[]{:S(2)}) copy-start(f32[128,16,128]{2,1,0:T(8,128)S(1)} %copy.178) | copy-start | bytes 3145732
  156.1 9.7 %copy-start.4 = (f32[128,16,128]{2,1,0:T(8,128)}, f32[128,16,128]{2,1,0:T(8,128)S(1)}, u32[]{:S(2)}) copy-start(f32[128,16,128]{2,1,0:T(8,128)S(1)} %copy.177) | copy-start | bytes 3145732
  180.6 1.0 copy-start.13
  180.6 2.0 copy-start.8
  190.6 2.9 copy-start.7
Sparse Core Ops, SparseCore 0:
  180.7 228.4 all-reduce.2
